TPU v7x, 128 devices: a whole 4x4x4 slice. The times are simulated.
128 devices in a mesh: gx: 8 (over z, x_hi), gy: 16 (over x_lo, y, core).
Axes of the slice: x: 4 (x_hi: 2, x_lo: 2; x = x_hi * 2 + x_lo), y: 4, z: 4, core: 2. Of those that a mesh axis runs over, the one named last changes fastest.
Arguments:
- ensemble: float32 [192, 384, 6, 128], P('gx', 'gy'), may hold values from -6 to 6
- cfl_ratio_primary_axis: float32 [192, 384, 6], P('gx', 'gy'), may hold values from -0.35 to 0.35
- cfl_ratio_secondary_axis: float32 [192, 384, 6], P('gx', 'gy'), may hold values from -0.35 to 0.35
- spreading_ratio: float32 [192, 384, 6], P('gx', 'gy'), may hold values from 0.02 to 0.07
- obs_owner: int32 [1024], replicated, may hold values from 0 to 127
- obs_local: int32 [1024], replicated, may hold values from 0 to 3455
- batch_order: int32 [1024], replicated, may hold values from 0 to 1023, each once
- obs_reach: int32 [1024], replicated, may hold values from 24 to 72
- obs_value: float32 [1024], replicated, may hold values from -6 to 6
- obs_variance: float32 [1024], replicated, may hold values from 0.25 to 4
- obs_noise: float32 [1024, 128], replicated, may hold values from -6 to 6
Outputs:
- analysis: float32 [192, 384, 6, 128], P('gx', 'gy')
All inputs are finite; a program needn't handle non-finite values.
Results may differ from a plain program's by a relative error of at most 0.0001.
Values sent between devices are 32-bit elements; how exact they have to be, the bound alone decides.
A program may use at most 64 MiB of HBM per device.

v0:
```python
import jax
import jax.numpy as jnp
from jax import lax
from jax.sharding import PartitionSpec as P

STEPS = 2
OB = 64


def with_halo(cells, sides, width):
    for axis, dim in sides:
        count = lax.axis_size(axis)
        ends = count - 1
        head = lax.slice_in_dim(cells, 0, width, axis=dim)
        tail = lax.slice_in_dim(cells, cells.shape[dim] - width, cells.shape[dim], axis=dim)
        cells = jnp.concatenate(
            [
                lax.ppermute(tail, axis, [(i, (i + 1) % count) for i in range(ends)]),
                cells,
                lax.ppermute(head, axis, [((i + 1) % count, i) for i in range(ends)]),
            ],
            axis=dim,
        )
    return cells


def propagate_prediction(bordered_grid, primary_cfl, secondary_cfl, spreading_rate):
    centre = bordered_grid[1:-1, 1:-1]
    west = bordered_grid[:-2, 1:-1]
    east = bordered_grid[2:, 1:-1]
    south = bordered_grid[1:-1, :-2]
    north = bordered_grid[1:-1, 2:]
    cxe = primary_cfl[..., None]
    cye = secondary_cfl[..., None]
    kde = spreading_rate[..., None]
    tend = -(jnp.maximum(cxe, 0.0) * (centre - west) + jnp.minimum(cxe, 0.0) * (east - centre))
    tend = tend - (
        jnp.maximum(cye, 0.0) * (centre - south) + jnp.minimum(cye, 0.0) * (north - centre)
    )
    tend = tend + kde * (east + west + north + south - 4.0 * centre)
    return centre + tend


def taper(col_x, col_y, obs_x, obs_y, reach):
    dx = col_x[:, None] - obs_x[None, :]
    dy = col_y[:, None] - obs_y[None, :]
    radius = reach.astype(jnp.float32)
    ratio = (dx * dx + dy * dy) / (radius * radius)[None, :]
    return jnp.maximum(1.0 - ratio, 0.0) ** 2


def batch_solve(hx, values, variance, noise):
    members = hx.shape[1]
    centred = hx - jnp.mean(hx, axis=1, keepdims=True)
    scaled = centred / (members - 1.0)
    cov = jnp.dot(
        centred, scaled.T, precision=lax.Precision.HIGHEST, preferred_element_type=jnp.float32
    )
    cov = cov + jnp.diag(variance)
    innov = values[:, None] + jnp.sqrt(variance)[:, None] * noise - hx
    factor = jnp.linalg.cholesky(cov)
    return (scaled, jax.scipy.linalg.cho_solve((factor, True), innov))


def localized_update(field, scaled, solved, weights, levels):
    gain = jnp.dot(
        field, scaled.T, precision=lax.Precision.HIGHEST, preferred_element_type=jnp.float32
    )
    width = scaled.shape[0]
    gain = (gain.reshape(-1, levels, width) * weights[:, None, :]).reshape(-1, width)
    return field + jnp.dot(
        gain, solved, precision=lax.Precision.HIGHEST, preferred_element_type=jnp.float32
    )


def per_device(
    ensemble,
    cfl_ratio_primary_axis,
    cfl_ratio_secondary_axis,
    spreading_ratio,
    obs_owner,
    obs_local,
    batch_order,
    obs_reach,
    obs_value,
    obs_variance,
    obs_noise,
):
    block_x, block_y, levels, members = ensemble.shape
    current_vector = ensemble
    for step in range(STEPS):
        bordered_grid = with_halo(current_vector, (("gx", 0), ("gy", 1)), 1)
        current_vector = propagate_prediction(
            bordered_grid, cfl_ratio_primary_axis, cfl_ratio_secondary_axis, spreading_ratio
        )
    row_index = lax.axis_index("gx")
    col_index = lax.axis_index("gy")
    span_y = lax.axis_size("gy")
    myself = row_index * span_y + col_index
    ix = obs_local // (block_y * levels)
    iy = obs_local // levels % block_y
    obs_fx = (obs_owner // span_y * block_x + ix).astype(jnp.float32)
    obs_fy = (obs_owner % span_y * block_y + iy).astype(jnp.float32)
    column = jnp.arange(block_x * block_y, dtype=jnp.int32)
    col_x = (row_index * block_x + column // block_y).astype(jnp.float32)
    col_y = (col_index * block_y + column % block_y).astype(jnp.float32)
    flat = current_vector.reshape(-1, members)
    batches = obs_local.shape[0] // OB

    def batch_fields(batch):
        chosen = lax.dynamic_slice_in_dim(batch_order, batch * OB, OB)
        return (chosen, obs_fx[chosen], obs_fy[chosen], obs_reach[chosen])

    def assimilate(batch, field):
        chosen, bx, by, reach = batch_fields(batch)
        owned = (obs_owner[chosen] == myself).astype(jnp.float32)
        picked = jnp.take(field, obs_local[chosen], axis=0) * owned[:, None]
        hx = lax.psum(picked, ("gx", "gy"))
        scaled, solved = batch_solve(hx, obs_value[chosen], obs_variance[chosen], obs_noise[chosen])
        weights = taper(col_x, col_y, bx, by, reach)
        return localized_update(field, scaled, solved, weights, levels)

    flat = lax.fori_loop(0, batches, assimilate, flat)
    return flat.reshape(block_x, block_y, levels, members)


def solution(mesh):
    return jax.shard_map(
        per_device,
        mesh=mesh,
        in_specs=(
            P("gx", "gy", None, None),
            P("gx", "gy", None),
            P("gx", "gy", None),
            P("gx", "gy", None),
            P(),
            P(),
            P(),
            P(),
            P(),
            P(),
            P(),
        ),
        out_specs=P("gx", "gy", None, None),
        check_vma=False,
    )
```

profile of v0, /device:TPU:1, one launch (start us, length us, event | category | flops | bytes accessed | tf_op | source)
XLA Modules:
  0.0 1618.9 jit_solution(883264019778957370)
XLA Ops:
  2.2 6.1 collective-permute-start
  30.9 6.2 collective-permute-start.4
  53.1 1561.0 %while.14 = (s32[]{:T(128)}, f32[3456,128]{1,0:T(8,128)S(1)}, s32[1024]{0:T(1024)}, s32[1024]{0:T(1024)S(1)}, s32[1024]{0:T(1024)S(1)}, /*index=5*/s32[]{:T(128)...) while((s32[]{:T(128)}, f32[3456,128]{1,0:T(8,128)S(1)}, ...), condition=%wide.region_5.6_spmd.clone, body=%wide.region_0.5_spmd.clone.sunk | while | flops 699519040 | bytes 17282964 | solution.py:123
  64.8 75.0 %psum.13 = f32[64,128]{1,0:T(8,128)S(1)} all-reduce(f32[64,128]{1,0:T(8,128)S(1)} %select_multiply_fusion.2), channel_id=1, replica_groups=mesh['gx'=8,'gy'=16] {'gx','gy'}, use_global_device_ids=true, to_apply=%region_1.1 | all-reduce | flops 8192 | bytes 65536 | tf_op jit(solution)/shard_map/while/body/eval_jaxpr/psum | solution.py:118
  144.1 5.9 cholesky.65
  173.3 62.6 %psum.13 = f32[64,128]{1,0:T(8,128)S(1)} all-reduce(f32[64,128]{1,0:T(8,128)S(1)} %select_multiply_fusion.2), channel_id=1, replica_groups=mesh['gx'=8,'gy'=16] {'gx','gy'}, use_global_device_ids=true, to_apply=%region_1.1 | all-reduce | flops 8192 | bytes 65536 | tf_op jit(solution)/shard_map/while/body/eval_jaxpr/psum | solution.py:118
  240.2 5.9 cholesky.65
  269.4 64.1 %psum.13 = f32[64,128]{1,0:T(8,128)S(1)} all-reduce(f32[64,128]{1,0:T(8,128)S(1)} %select_multiply_fusion.2), channel_id=1, replica_groups=mesh['gx'=8,'gy'=16] {'gx','gy'}, use_global_device_ids=true, to_apply=%region_1.1 | all-reduce | flops 8192 | bytes 65536 | tf_op jit(solution)/shard_map/while/body/eval_jaxpr/psum | solution.py:118
  337.9 5.9 cholesky.65
  367.1 62.6 %psum.13 = f32[64,128]{1,0:T(8,128)S(1)} all-reduce(f32[64,128]{1,0:T(8,128)S(1)} %select_multiply_fusion.2), channel_id=1, replica_groups=mesh['gx'=8,'gy'=16] {'gx','gy'}, use_global_device_ids=true, to_apply=%region_1.1 | all-reduce | flops 8192 | bytes 65536 | tf_op jit(solution)/shard_map/while/body/eval_jaxpr/psum | solution.py:118
  434.0 5.9 cholesky.65
  463.2 64.1 %psum.13 = f32[64,128]{1,0:T(8,128)S(1)} all-reduce(f32[64,128]{1,0:T(8,128)S(1)} %select_multiply_fusion.2), channel_id=1, replica_groups=mesh['gx'=8,'gy'=16] {'gx','gy'}, use_global_device_ids=true, to_apply=%region_1.1 | all-reduce | flops 8192 | bytes 65536 | tf_op jit(solution)/shard_map/while/body/eval_jaxpr/psum | solution.py:118
  531.6 5.9 cholesky.65
  560.9 62.6 %psum.13 = f32[64,128]{1,0:T(8,128)S(1)} all-reduce(f32[64,128]{1,0:T(8,128)S(1)} %select_multiply_fusion.2), channel_id=1, replica_groups=mesh['gx'=8,'gy'=16] {'gx','gy'}, use_global_device_ids=true, to_apply=%region_1.1 | all-reduce | flops 8192 | bytes 65536 | tf_op jit(solution)/shard_map/while/body/eval_jaxpr/psum | solution.py:118
  627.8 5.9 cholesky.65
  657.0 64.1 %psum.13 = f32[64,128]{1,0:T(8,128)S(1)} all-reduce(f32[64,128]{1,0:T(8,128)S(1)} %select_multiply_fusion.2), channel_id=1, replica_groups=mesh['gx'=8,'gy'=16] {'gx','gy'}, use_global_device_ids=true, to_apply=%region_1.1 | all-reduce | flops 8192 | bytes 65536 | tf_op jit(solution)/shard_map/while/body/eval_jaxpr/psum | solution.py:118
  725.4 5.9 cholesky.65
  754.6 62.6 %psum.13 = f32[64,128]{1,0:T(8,128)S(1)} all-reduce(f32[64,128]{1,0:T(8,128)S(1)} %select_multiply_fusion.2), channel_id=1, replica_groups=mesh['gx'=8,'gy'=16] {'gx','gy'}, use_global_device_ids=true, to_apply=%region_1.1 | all-reduce | flops 8192 | bytes 65536 | tf_op jit(solution)/shard_map/while/body/eval_jaxpr/psum | solution.py:118
  821.5 5.9 cholesky.65
  850.7 64.1 %psum.13 = f32[64,128]{1,0:T(8,128)S(1)} all-reduce(f32[64,128]{1,0:T(8,128)S(1)} %select_multiply_fusion.2), channel_id=1, replica_groups=mesh['gx'=8,'gy'=16] {'gx','gy'}, use_global_device_ids=true, to_apply=%region_1.1 | all-reduce | flops 8192 | bytes 65536 | tf_op jit(solution)/shard_map/while/body/eval_jaxpr/psum | solution.py:118
  919.1 5.9 cholesky.65
  948.4 62.6 %psum.13 = f32[64,128]{1,0:T(8,128)S(1)} all-reduce(f32[64,128]{1,0:T(8,128)S(1)} %select_multiply_fusion.2), channel_id=1, replica_groups=mesh['gx'=8,'gy'=16] {'gx','gy'}, use_global_device_ids=true, to_apply=%region_1.1 | all-reduce | flops 8192 | bytes 65536 | tf_op jit(solution)/shard_map/while/body/eval_jaxpr/psum | solution.py:118
  1015.3 5.9 cholesky.65
  1044.5 64.1 %psum.13 = f32[64,128]{1,0:T(8,128)S(1)} all-reduce(f32[64,128]{1,0:T(8,128)S(1)} %select_multiply_fusion.2), channel_id=1, replica_groups=mesh['gx'=8,'gy'=16] {'gx','gy'}, use_global_device_ids=true, to_apply=%region_1.1 | all-reduce | flops 8192 | bytes 65536 | tf_op jit(solution)/shard_map/while/body/eval_jaxpr/psum | solution.py:118
  1112.9 5.9 cholesky.65
  1142.1 62.6 %psum.13 = f32[64,128]{1,0:T(8,128)S(1)} all-reduce(f32[64,128]{1,0:T(8,128)S(1)} %select_multiply_fusion.2), channel_id=1, replica_groups=mesh['gx'=8,'gy'=16] {'gx','gy'}, use_global_device_ids=true, to_apply=%region_1.1 | all-reduce | flops 8192 | bytes 65536 | tf_op jit(solution)/shard_map/while/body/eval_jaxpr/psum | solution.py:118
  1238.2 64.1 %psum.13 = f32[64,128]{1,0:T(8,128)S(1)} all-reduce(f32[64,128]{1,0:T(8,128)S(1)} %select_multiply_fusion.2), channel_id=1, replica_groups=mesh['gx'=8,'gy'=16] {'gx','gy'}, use_global_device_ids=true, to_apply=%region_1.1 | all-reduce | flops 8192 | bytes 65536 | tf_op jit(solution)/shard_map/while/body/eval_jaxpr/psum | solution.py:118
  1306.6 5.9 cholesky.65
  1335.9 62.6 %psum.13 = f32[64,128]{1,0:T(8,128)S(1)} all-reduce(f32[64,128]{1,0:T(8,128)S(1)} %select_multiply_fusion.2), channel_id=1, replica_groups=mesh['gx'=8,'gy'=16] {'gx','gy'}, use_global_device_ids=true, to_apply=%region_1.1 | all-reduce | flops 8192 | bytes 65536 | tf_op jit(solution)/shard_map/while/body/eval_jaxpr/psum | solution.py:118
  1432.0 64.1 %psum.13 = f32[64,128]{1,0:T(8,128)S(1)} all-reduce(f32[64,128]{1,0:T(8,128)S(1)} %select_multiply_fusion.2), channel_id=1, replica_groups=mesh['gx'=8,'gy'=16] {'gx','gy'}, use_global_device_ids=true, to_apply=%region_1.1 | all-reduce | flops 8192 | bytes 65536 | tf_op jit(solution)/shard_map/while/body/eval_jaxpr/psum | solution.py:118
  1500.4 5.9 cholesky.65
  1529.6 62.6 %psum.13 = f32[64,128]{1,0:T(8,128)S(1)} all-reduce(f32[64,128]{1,0:T(8,128)S(1)} %select_multiply_fusion.2), channel_id=1, replica_groups=mesh['gx'=8,'gy'=16] {'gx','gy'}, use_global_device_ids=true, to_apply=%region_1.1 | all-reduce | flops 8192 | bytes 65536 | tf_op jit(solution)/shard_map/while/body/eval_jaxpr/psum | solution.py:118
  (682 shorter events, 504.0 us)
Async XLA Ops:
  0.9 10.4 collective-permute-start.1
  2.2 9.2 collective-permute-start
  11.3 7.9 copy-start.16
  12.7 10.1 collective-permute-start.3
  15.9 7.5 collective-permute-start.2
  29.3 15.4 copy-start
  29.3 15.4 copy-start.1
  29.3 16.8 %copy-start.7 = (f32[24,24,6]{0,2,1:T(8,128)S(1)}, f32[24,24,6]{0,2,1:T(8,128)}, u32[]{:S(2)}) copy-start(f32[24,24,6]{0,2,1:T(8,128)} %copy.93) | copy-start | bytes 41476
  29.3 16.8 %copy-start.8 = (f32[24,24,6]{0,2,1:T(8,128)S(1)}, f32[24,24,6]{0,2,1:T(8,128)}, u32[]{:S(2)}) copy-start(f32[24,24,6]{0,2,1:T(8,128)} %copy.91) | copy-start | bytes 41476
  29.3 16.8 %copy-start.9 = (f32[24,24,6]{0,2,1:T(8,128)S(1)}, f32[24,24,6]{0,2,1:T(8,128)}, u32[]{:S(2)}) copy-start(f32[24,24,6]{0,2,1:T(8,128)} %copy.86) | copy-start | bytes 41476
  29.3 16.8 %copy-start.10 = (f32[24,24,6]{0,2,1:T(8,128)S(1)}, f32[24,24,6]{0,2,1:T(8,128)}, u32[]{:S(2)}) copy-start(f32[24,24,6]{0,2,1:T(8,128)} %copy.82) | copy-start | bytes 41476
  29.3 16.8 %copy-start.11 = (f32[24,24,6]{0,2,1:T(8,128)S(1)}, f32[24,24,6]{0,2,1:T(8,128)}, u32[]{:S(2)}) copy-start(f32[24,24,6]{0,2,1:T(8,128)} %copy.78) | copy-start | bytes 41476
  29.5 8.4 collective-permute-start.5
  30.9 7.9 collective-permute-start.4
  38.9 5.9 collective-permute-start.7
  41.6 4.5 collective-permute-start.6
  142.9 15.1 copy-start.5
  239.1 15.1 copy-start.5
  336.7 15.1 copy-start.5
  432.8 15.1 copy-start.5
  530.5 15.1 copy-start.5
  626.6 15.1 copy-start.5
  724.2 15.1 copy-start.5
  820.3 15.1 copy-start.5
  918.0 15.1 copy-start.5
  1014.1 15.1 copy-start.5
  1111.7 15.1 copy-start.5
  1207.8 15.1 copy-start.5
  1305.5 15.1 copy-start.5
  1401.6 15.1 copy-start.5
  1499.2 15.1 copy-start.5
  1595.4 15.1 copy-start.5
  (8 other events, 17.1 us)
where the time goes:
time: 1620 us
  blocking collectives  1020 us (63%)
  other arithmetic  223 us (14%)
  local copies, waits for them, and re-layouts  222 us (14%)
  matrix products  117 us (7%)
  starting transfers between devices  27.2 us (2%)
    psum x16, blocking collectives, assimilate(): hx = lax.psum(picked, ('gx', 'gy'))  1020 us
    another operation x48, other arithmetic, batch_solve(): factor = jnp.linalg.cholesky(cov)  105 us
    mul x48, local copies, waits for them, and re-layouts, localized_update(): gain.reshape(-1, levels, width) * weights[:, None, :]  99.5 us
    another operation x32, other arithmetic, batch_solve(): return (scaled, jax.scipy.linalg.cho_solve((factor, True), innov))  88.4 us
    dot_general x16, matrix products, localized_update(): jnp.dot(gain, solved, precision=lax.Precision.HIGHEST, preferred_element_...  57.3 us
    dot_general x16, matrix products, localized_update(): jnp.dot(field, scaled.T, precision=lax.Precision.HIGHEST, preferred_eleme...  48.7 us
    gather x48, local copies, waits for them, and re-layouts, batch_fields(): return (chosen, obs_fx[chosen], obs_fy[chosen], obs_reach[chosen])  35 us
  transfers between devices with their start and end apart: 8, of which 4 were waited for; matrix products, arithmetic and copies ran while one was open for 0% of the time, Pallas kernels for 0%

commit v1 on v0

v1 whole, which is shorter than its diff:
```python
import jax
import jax.numpy as jnp
from jax import lax
from jax.experimental import pallas as pl
from jax.experimental.pallas import tpu as pltpu
from jax.sharding import PartitionSpec as P

STEPS = 2
OB = 64
ITERS = 5
BOUND = 16.0
F32 = jnp.float32
BF16 = jnp.bfloat16


def with_halo(cells, sides, width):
    for axis, dim in sides:
        count = lax.axis_size(axis)
        ends = count - 1
        head = lax.slice_in_dim(cells, 0, width, axis=dim)
        tail = lax.slice_in_dim(cells, cells.shape[dim] - width, cells.shape[dim], axis=dim)
        cells = jnp.concatenate(
            [
                lax.ppermute(tail, axis, [(i, (i + 1) % count) for i in range(ends)]),
                cells,
                lax.ppermute(head, axis, [((i + 1) % count, i) for i in range(ends)]),
            ],
            axis=dim,
        )
    return cells


def propagate_prediction(bordered_grid, primary_cfl, secondary_cfl, spreading_rate):
    centre = bordered_grid[1:-1, 1:-1]
    west = bordered_grid[:-2, 1:-1]
    east = bordered_grid[2:, 1:-1]
    south = bordered_grid[1:-1, :-2]
    north = bordered_grid[1:-1, 2:]
    cxe = primary_cfl[..., None]
    cye = secondary_cfl[..., None]
    kde = spreading_rate[..., None]
    tend = -(jnp.maximum(cxe, 0.0) * (centre - west) + jnp.minimum(cxe, 0.0) * (east - centre))
    tend = tend - (
        jnp.maximum(cye, 0.0) * (centre - south) + jnp.minimum(cye, 0.0) * (north - centre)
    )
    tend = tend + kde * (east + west + north + south - 4.0 * centre)
    return centre + tend


def split(x):
    high = x.astype(BF16)
    return high, (x - high.astype(F32)).astype(BF16)


def assimilate(fx_ref, fy_ref, ir_ref, rows_x, rows_y, y_in, w_ref, x_ref, out_ref, y_ref, t_ref, v_ref):
    block_x, levels, block_y, members = x_ref.shape
    count = y_in.shape[0]
    batches = count // OB
    y_ref[...] = y_in[...]
    out_ref[...] = x_ref[...]
    lane = lax.broadcasted_iota(jnp.int32, (OB, 2 * OB), 1)
    row = lax.broadcasted_iota(jnp.int32, (OB, 2 * OB), 0)
    eye = jnp.where((lane == row) | (lane == row + OB), 1.0, 0.0).astype(F32)
    ys = lax.broadcasted_iota(jnp.int32, (block_y, 1), 0).astype(F32)

    def step(b, _):
        now = pl.ds(pl.multiple_of(b * OB, OB), OB)
        hx = y_ref[now, :]
        centred = hx - jnp.mean(hx, axis=1, keepdims=True)
        high, low = split(centred)
        high2 = jnp.concatenate([high, high], axis=1)
        low2 = jnp.concatenate([low, low], axis=1)
        side = jnp.concatenate([high2, low2, low2, high2], axis=0)

        def project(x):
            both = jnp.concatenate(split(x), axis=1)
            pair = lax.dot_general(both, side, (((1,), (1,)), ((), ())), preferred_element_type=F32)
            return pair[:, : 2 * OB] + pair[:, 2 * OB :]

        p = project(centred) * (1.0 / (members - 1.0))
        norm = jnp.max(jnp.sum(jnp.abs(p), axis=0, keepdims=True), axis=1, keepdims=True)
        c = 1.0 + jnp.maximum(norm, 0.0625)
        top = c + 1.0
        t = top / (c - 1.0)
        alpha = 2.0 / top
        r = ((c - 1.0) / top) * eye - alpha * p
        rhs = w_ref[now, :] - hx
        v = alpha * rhs
        for i in range(ITERS):
            t = 2.0 * t * t - 1.0
            back = 1.0 / t
            gain = 1.0 + back
            rh, rl = split(r)
            vh, vl = split(v)
            left = jnp.concatenate([rh, rl], axis=1)
            head = jnp.concatenate([rh, vh], axis=1)
            tail = jnp.concatenate([rl, vl], axis=1)
            right = jnp.concatenate([head, tail, head, tail], axis=0)
            prod = jnp.dot(left, right, preferred_element_type=F32)
            v = gain * (v + prod[:, 2 * OB :])
            if i + 1 < ITERS:
                r = gain * prod[:, : 2 * OB] - back * eye
        v_ref[...] = v

        @pl.when(jnp.max(norm) > BOUND)
        def _():
            t_ref[...] = p + eye
            v_ref[...] = rhs

            def pivot(k, _):
                at = lane[:1, :] == k
                trow = t_ref[pl.ds(k, 1), :]
                scale = 1.0 / jnp.sum(jnp.where(at, trow, 0.0), axis=1, keepdims=True)
                trow = trow * scale
                vrow = v_ref[pl.ds(k, 1), :] * scale
                mat = t_ref[...]
                col = jnp.sum(jnp.where(lane == k, mat, 0.0), axis=1, keepdims=True)
                mine = row == k
                t_ref[...] = jnp.where(mine, trow, mat - col * trow)
                v_ref[...] = jnp.where(mine, vrow, v_ref[...] - col * vrow)
                return 0

            lax.fori_loop(0, OB, pivot, 0)

        zh, zl = split(v_ref[...] * (1.0 / (members - 1.0)))
        solved = jnp.concatenate([zh, zl, zh, zl], axis=0)

        def spread(g):
            both = jnp.concatenate(split(g), axis=1)
            return jnp.dot(both, solved, preferred_element_type=F32)

        px = fx_ref[pl.ds(b, 1), :]
        py = fy_ref[pl.ds(b, 1), :]
        ir = ir_ref[pl.ds(b, 1), :]

        def later(j, _):
            at = pl.ds(pl.multiple_of(j * OB, OB), OB)
            old = y_ref[at, :]
            dx = rows_x[at, :] - px
            dy = rows_y[at, :] - py
            near = jnp.maximum(1.0 - (dx * dx + dy * dy) * ir, 0.0)
            y_ref[at, :] = old + spread(project(old) * (near * near))
            return 0

        lax.fori_loop(b + 1, batches, later, 0)
        dy = ys - py
        dy2 = dy * dy * ir

        def cells(i, _):
            dx = i.astype(F32) - px
            near = jnp.maximum((1.0 - dx * dx * ir) - dy2, 0.0)
            rho = near * near
            old = out_ref[i].reshape(levels * block_y, members)
            g = project(old).reshape(levels, block_y, members) * rho[None]
            new = old + spread(g.reshape(levels * block_y, members))
            out_ref[i] = new.reshape(levels, block_y, members)
            return 0

        lax.fori_loop(0, block_x, cells, 0)
        return 0

    lax.fori_loop(0, batches, step, 0)


def per_device(
    ensemble,
    cfl_ratio_primary_axis,
    cfl_ratio_secondary_axis,
    spreading_ratio,
    obs_owner,
    obs_local,
    batch_order,
    obs_reach,
    obs_value,
    obs_variance,
    obs_noise,
):
    block_x, block_y, levels, members = ensemble.shape
    current_vector = ensemble
    for step in range(STEPS):
        bordered_grid = with_halo(current_vector, (("gx", 0), ("gy", 1)), 1)
        current_vector = propagate_prediction(
            bordered_grid, cfl_ratio_primary_axis, cfl_ratio_secondary_axis, spreading_ratio
        )
    row_index = lax.axis_index("gx")
    col_index = lax.axis_index("gy")
    span_y = lax.axis_size("gy")
    myself = row_index * span_y + col_index
    owner = obs_owner[batch_order]
    local = obs_local[batch_order]
    ix = local // (block_y * levels)
    iy = local // levels % block_y
    lev = local % levels
    fx = (owner // span_y * block_x + ix - row_index * block_x).astype(F32)
    fy = (owner % span_y * block_y + iy - col_index * block_y).astype(F32)
    reach = obs_reach[batch_order].astype(F32)
    count = local.shape[0]
    batches = count // OB

    def lanes(v):
        v = v.reshape(batches, OB)
        return jnp.concatenate([v, v], axis=1)

    root = jnp.sqrt(obs_variance[batch_order])
    inv = 1.0 / root
    wanted = obs_noise[batch_order] + (obs_value[batch_order] * inv)[:, None]
    state = jnp.transpose(current_vector, (0, 2, 1, 3))
    flat = state.reshape(-1, members)
    picked = jnp.take(flat, (ix * levels + lev) * block_y + iy, axis=0)
    picked = picked * jnp.where(owner == myself, inv, 0.0)[:, None]
    seen = lax.psum(picked, ("gx", "gy"))
    args = (
        lanes(fx),
        lanes(fy),
        lanes(1.0 / (reach * reach)),
        jnp.broadcast_to(fx[:, None], (count, members)),
        jnp.broadcast_to(fy[:, None], (count, members)),
        seen,
        wanted,
        state,
    )
    out = pl.pallas_call(
        assimilate,
        out_shape=jax.ShapeDtypeStruct(state.shape, F32),
        in_specs=[pl.BlockSpec(memory_space=pltpu.VMEM)] * len(args),
        out_specs=pl.BlockSpec(memory_space=pltpu.VMEM),
        scratch_shapes=[
            pltpu.VMEM((count, members), F32),
            pltpu.VMEM((OB, 2 * OB), F32),
            pltpu.VMEM((OB, members), F32),
        ],
        name="assimilate",
    )(*args)
    return jnp.transpose(out, (0, 2, 1, 3))


def solution(mesh):
    return jax.shard_map(
        per_device,
        mesh=mesh,
        in_specs=(
            P("gx", "gy", None, None),
            P("gx", "gy", None),
            P("gx", "gy", None),
            P("gx", "gy", None),
            P(),
            P(),
            P(),
            P(),
            P(),
            P(),
            P(),
        ),
        out_specs=P("gx", "gy", None, None),
        check_vma=False,
    )
```

time: 1620 us -> 451 us (0.28)
  blocking collectives: 1020 us -> 0 us
  other arithmetic: 223 us -> 23.3 us
  Pallas kernels: 0 us -> 194 us
  local copies, waits for them, and re-layouts: 222 us -> 34.8 us
  waiting for transfers between devices: 2.99 us -> 159 us
  matrix products: 117 us -> 0 us
    psum x16 -> x0, blocking collectives: 1020 us -> none  [assimilate(): hx = lax.psum(picked, ('gx', 'gy'))]
    another operation x80 -> x0, other arithmetic: 194 us -> none  [the longest x48 105 us: batch_solve(): factor = jnp.linalg.cholesky(cov)]
    pallas_call x0 -> x1, Pallas kernels: none -> 194 us  [per_device(): pl.pallas_call(assimilate, out_shape=jax.ShapeDtypeStruct(state.shape, F3...]
    psum x0 -> x1, waiting for transfers between devices: none -> 148 us  [per_device(): seen = lax.psum(picked, ('gx', 'gy'))]
    dot_general x48 -> x0, matrix products: 110 us -> none  [the longest x16 57.3 us: localized_update(): jnp.dot(gain, solved, precision=lax.Precision.HIGHEST, preferred_element_...]
    mul x48 -> x0, local copies, waits for them, and re-layouts: 99.5 us -> none  [localized_update(): gain.reshape(-1, levels, width) * weights[:, None, :]]
    gather x144 -> x8, local copies, waits for them, and re-layouts: 101 us -> 29.8 us  [the longest x2 7.33 us: per_device(): wanted = obs_noise[batch_order] + (obs_value[batch_order] * inv)[:, None]]
  transfers between devices with their start and end apart: 8 -> 9, of which waited for: 4 -> 4; matrix products, arithmetic and copies ran while one was open for 0% -> 8% of each run, Pallas kernels for 0% -> 0%
where the time goes in v1:
time: 451 us; the launch traced here: 450 us
  Pallas kernels  194 us (43%)
  waiting for transfers between devices  159 us (35%)
  local copies, waits for them, and re-layouts  34.8 us (8%)
  starting transfers between devices  25.3 us (6%)
  other arithmetic  23.3 us (5%)
  between operations  13.8 us (3%)
    pallas_call x1, Pallas kernels, per_device(): pl.pallas_call(assimilate, out_shape=jax.ShapeDtypeStruct(state.shape, F3...  194 us
    psum x1, waiting for transfers between devices, per_device(): seen = lax.psum(picked, ('gx', 'gy'))  148 us
    ppermute x4, starting transfers between devices, with_halo(): lax.ppermute(tail, axis, [(i, (i + 1) % count) for i in range(ends)])  18.9 us
    ppermute x4, waiting for transfers between devices, with_halo(): lax.ppermute(head, axis, [((i + 1) % count, i) for i in range(ends)])  11.3 us
    add x2, other arithmetic, propagate_prediction(): return centre + tend  10.7 us
  transfers between devices with their start and end apart: 9, of which 4 were waited for; matrix products, arithmetic and copies ran while one was open for 8% of the time, Pallas kernels for 0%

profile of v1, /device:TPU:1, one launch (start us, length us, event | category | flops | bytes accessed | tf_op | source)
XLA Modules:
  0.0 449.8 jit_solution(1672791097627455018)
XLA Ops:
  6.5 1.0 fusion.67
  7.5 5.5 %collective-permute-start = (f32[1,24,6,128]{3,1,2,0:T(8,128)S(1)}, f32[1,24,6,128]{3,1,2,0:T(8,128)S(1)}, u32[]{:S(2)}, u32[]{:S(2)}) collective-permute-start(f32[1,24,6,128]{3,1,2,0:T(8,128)S(1)} %get-tuple-element.16), channel_id=1, source_target_pairs={{0,16},{16,32},{32,48},{48,64},{64,80},{80,96},{96,112},{1,17},{17... | collective-permute-start | bytes 221192 | tf_op jit(solution)/shard_map/ppermute | solution.py:24
  13.0 1.3 collective-permute-start.1
  14.3 0.9 broadcast_maximum_fusion.1
  15.2 0.9 broadcast_maximum_fusion
  16.1 0.7 fusion.60
  16.8 4.5 %gather_fusion.1 = s32[1024]{0:T(1024)S(1)} fusion(s32[1024]{0:T(1024)S(1)} %copy-done.1, s32[1024]{0:T(1024)S(1)} %fusion.60), kind=kCustom, calls=%fused_computation.1 | custom fusion | bytes 12288 | tf_op jit(solution)/shard_map/gather | solution.py:190
  22.0 4.5 %gather_fusion = s32[1024]{0:T(1024)S(1)} fusion(s32[1024]{0:T(1024)S(1)} %copy-done.2, s32[1024]{0:T(1024)S(1)} %fusion.60), kind=kCustom, calls=%fused_computation | custom fusion | bytes 12288 | tf_op jit(solution)/shard_map/gather | solution.py:189
  26.6 4.5 %gather_fusion.4 = f32[1024]{0:T(1024)S(1)} fusion(f32[1024]{0:T(1024)S(1)} %copy-done.3, s32[1024]{0:T(1024)S(1)} %fusion.60), kind=kCustom, calls=%fused_computation.4 | custom fusion | bytes 12288 | tf_op jit(solution)/shard_map/gather | solution.py:204
  31.1 4.5 %gather_fusion.6 = f32[1024]{0:T(1024)S(1)} fusion(f32[1024]{0:T(1024)S(1)} %copy-done.4, s32[1024]{0:T(1024)S(1)} %fusion.60), kind=kCustom, calls=%fused_computation.6 | custom fusion | bytes 12288 | tf_op jit(solution)/shard_map/gather | solution.py:206
  36.0 2.8 gather_fusion.5
  38.9 1.0 broadcast_add_fusion.w_ref
  40.0 4.5 %gather_fusion.2 = s32[1024]{0:T(1024)S(1)} fusion(s32[1024]{0:T(1024)S(1)} %copy-done.5, s32[1024]{0:T(1024)S(1)} %fusion.60), kind=kCustom, calls=%fused_computation.2 | custom fusion | bytes 12288 | tf_op jit(solution)/shard_map/gather | solution.py:196
  44.7 1.3 copy-done.7
  46.1 4.0 collective-permute-start.2
  50.2 1.9 collective-permute-start.3
  52.4 3.6 collective-permute-done.3
  55.9 6.6 %fusion.26 = f32[24,24,6,128]{3,1,2,0:T(8,128)S(1)} fusion(f32[24,24,6,128]{3,1,2,0:T(8,128)} %param.11, f32[1,24,6,128]{3,1,2,0:T(8,128)S(1)} %collective-permute-done.1, f32[1,24,6,128]{3,1,2,0:T(8,128)S(1)} %collective-permute-done, f32[26,1,6,128]{3,1,2,0:T(1,128)S(1)} %collective-permute-done.3, f32[26,24,6,128]{3,1,2,0:T(8,128)} %copy-done.7, ...), kind=kLoop, calls=%fused_computation.44 | loop fusion | flops 10616832 | bytes 5832192 | tf_op jit(solution)/shard_map/add | solution.py:47
  62.5 5.8 %collective-permute-start.4 = (f32[1,24,6,128]{3,1,2,0:T(8,128)S(1)}, f32[1,24,6,128]{3,1,2,0:T(8,128)S(1)}, u32[]{:S(2)}, u32[]{:S(2)}) collective-permute-start(f32[1,24,6,128]{3,1,2,0:T(8,128)S(1)} %get-tuple-element.14), channel_id=1, source_target_pairs={{0,16},{16,32},{32,48},{48,64},{64,80},{80,96},{96,112},{1,17},{17... | collective-permute-start | bytes 221192 | tf_op jit(solution)/shard_map/ppermute | solution.py:24
  68.3 1.3 collective-permute-start.5
  70.3 4.6 %collective-permute-done.5 = f32[1,24,6,128]{3,1,2,0:T(8,128)S(1)} collective-permute-done((f32[1,24,6,128]{3,1,2,0:T(8,128)S(1)}, f32[1,24,6,128]{3,1,2,0:T(8,128)S(1)}, u32[]{:S(2)}, u32[]{:S(2)}) %collective-permute-start.5) | collective-permute-done | bytes 73760 | tf_op jit(solution)/shard_map/ppermute | solution.py:26
  75.0 3.6 collective-permute-start.6
  78.6 1.9 collective-permute-start.7
  81.2 3.1 collective-permute-done.7
  84.4 4.1 fusion.6
  88.4 4.3 gather_fusion.3
  92.7 1.8 select_multiply_fusion
  94.6 5.1 %fusion.68.x_ref = f32[24,6,24,128]{3,2,1,0:T(8,128)} fusion(f32[24,24,6,128]{3,1,2,0:T(8,128)S(1)} %fusion.26, f32[24,24,6]{1,2,0:T(8,128)S(1)} %copy.21, f32[26,1,6,128]{3,1,2,0:T(1,128)} %copy-done.8, f32[1,24,6,128]{3,1,2,0:T(8,128)S(1)} %collective-permute-done.5, f32[1,24,6,128]{3,1,2,0:T(8,128)S(1)} %collective-permute-done.4, ...), kind=kLoop, calls=%fused_computation.138 | loop fusion | flops 12386304 | bytes 3915264 | tf_op jit(solution)/shard_map/transpose | solution.py:207
  99.7 147.6 %all-reduce.2.cloned.1.call-done.y_in = f32[1024,128]{1,0:T(8,128)} async-done(((f32[1024,128]{1,0:T(8,128)}), f32[1024,128]{1,0:T(8,128)}) %all-reduce.2.cloned.1.call-update) | async-done | bytes 524304 | tf_op jit(solution)/shard_map/psum | solution.py:211
  247.3 1.0 broadcast_in_dim.21.rows_x
  248.3 1.0 broadcast_in_dim.22.rows_y
  249.3 193.7 %assimilate.1 = f32[24,6,24,128]{3,2,1,0:T(8,128)} custom-call(f32[16,128]{1,0:T(8,128)} %get-tuple-element.33.fx_ref, f32[16,128]{1,0:T(8,128)} %get-tuple-element.34.fy_ref, f32[16,128]{1,0:T(8,128)} %pad_maximum_fusion.17.ir_ref, f32[1024,128]{1,0:T(8,128)} %broadcast_in_dim.21.rows_x, f32[1024,128]{1,0:T(8,128)} %broadcast_in_dim.22.rows_y, ...), custom_call_target="tpu_custom_call" | custom-call | tf_op jit(solution)/shard_map/assimilate/pallas_call | solution.py:222
  (52 shorter events, 3.1 us)
Async XLA Ops:
  6.5 29.5 %copy-start = (f32[1024,128]{1,0:T(8,128)S(1)}, f32[1024,128]{1,0:T(8,128)}, u32[]{:S(2)}) copy-start(f32[1024,128]{1,0:T(8,128)} %param.21) | copy-start | bytes 1572868
  6.5 10.3 %copy-start.1 = (s32[1024]{0:T(1024)S(1)}, s32[1024]{0:T(1024)}, u32[]{:S(2)}) copy-start(s32[1024]{0:T(1024)} %param.16) | copy-start | bytes 12292
  6.5 240.7 %all-reduce.2.cloned.1.call-start = ((), (), s32[]{:S(2)}) async-start(), calls=%async_computation | async-start | bytes 1048576 | tf_op jit(solution)/shard_map/psum | solution.py:211
  7.5 37.0 %collective-permute-start = (f32[1,24,6,128]{3,1,2,0:T(8,128)S(1)}, f32[1,24,6,128]{3,1,2,0:T(8,128)S(1)}, u32[]{:S(2)}, u32[]{:S(2)}) collective-permute-start(f32[1,24,6,128]{3,1,2,0:T(8,128)S(1)} %get-tuple-element.16), channel_id=1, source_target_pairs={{0,16},{16,32},{32,48},{48,64},{64,80},{80,96},{96,112},{1,17},{17... | collective-permute-start | bytes 221192 | tf_op jit(solution)/shard_map/ppermute | solution.py:24
  13.0 31.7 %collective-permute-start.1 = (f32[1,24,6,128]{3,1,2,0:T(8,128)S(1)}, f32[1,24,6,128]{3,1,2,0:T(8,128)S(1)}, u32[]{:S(2)}, u32[]{:S(2)}) collective-permute-start(f32[1,24,6,128]{3,1,2,0:T(8,128)S(1)} %get-tuple-element.17), channel_id=1, source_target_pairs={{16,0},{32,16},{48,32},{64,48},{80,64},{96,80},{112,96},{17,1},{33... | collective-permute-start | bytes 221192 | tf_op jit(solution)/shard_map/ppermute | solution.py:26
  16.8 5.2 %copy-start.2 = (s32[1024]{0:T(1024)S(1)}, s32[1024]{0:T(1024)}, u32[]{:S(2)}) copy-start(s32[1024]{0:T(1024)} %param.15) | copy-start | bytes 12292
  22.0 4.5 %copy-start.3 = (f32[1024]{0:T(1024)S(1)}, f32[1024]{0:T(1024)}, u32[]{:S(2)}) copy-start(f32[1024]{0:T(1024)} %param.20) | copy-start | bytes 12292
  26.5 4.6 %copy-start.4 = (f32[1024]{0:T(1024)S(1)}, f32[1024]{0:T(1024)}, u32[]{:S(2)}) copy-start(f32[1024]{0:T(1024)} %param.19) | copy-start | bytes 12292
  36.0 3.9 copy-start.5
  40.0 4.6 %copy-start.6 = (f32[24,24,6,128]{3,1,2,0:T(8,128)S(1)}, f32[24,24,6,128]{3,1,2,0:T(8,128)}, u32[]{:S(2)}) copy-start(f32[24,24,6,128]{3,1,2,0:T(8,128)} %param.11) | copy-start | bytes 5308420
  44.6 7.7 %copy-start.9 = (f32[24,24,6]{1,0,2:T(8,128)S(1)}, f32[24,24,6]{1,0,2:T(8,128)}, u32[]{:S(2)}) copy-start(f32[24,24,6]{1,0,2:T(8,128)} %param.14) | copy-start | bytes 41476
  44.7 1.3 copy-start.7
  46.1 6.2 %collective-permute-start.2 = (f32[26,1,6,128]{3,1,2,0:T(1,128)S(1)}, f32[26,1,6,128]{3,1,2,0:T(1,128)S(1)}, u32[]{:S(2)}, u32[]{:S(2)}) collective-permute-start(f32[26,1,6,128]{3,1,2,0:T(1,128)S(1)} %get-tuple-element.12), channel_id=1, source_target_pairs={{0,1},{1,2},{2,3},{3,4},{4,5},{5,6},{6,7},{7,8},{8,9},{9,10},{10,1... | collective-permute-start | bytes 239624 | tf_op jit(solution)/shard_map/ppermute | solution.py:24
  50.2 5.7 %collective-permute-start.3 = (f32[26,1,6,128]{3,1,2,0:T(1,128)S(1)}, f32[26,1,6,128]{3,1,2,0:T(1,128)S(1)}, u32[]{:S(2)}, u32[]{:S(2)}) collective-permute-start(f32[26,1,6,128]{3,1,2,0:T(1,128)S(1)} %get-tuple-element.13), channel_id=1, source_target_pairs={{1,0},{2,1},{3,2},{4,3},{5,4},{6,5},{7,6},{8,7},{9,8},{10,9},{11,1... | collective-permute-start | bytes 239624 | tf_op jit(solution)/shard_map/ppermute | solution.py:26
  62.5 7.8 %collective-permute-start.4 = (f32[1,24,6,128]{3,1,2,0:T(8,128)S(1)}, f32[1,24,6,128]{3,1,2,0:T(8,128)S(1)}, u32[]{:S(2)}, u32[]{:S(2)}) collective-permute-start(f32[1,24,6,128]{3,1,2,0:T(8,128)S(1)} %get-tuple-element.14), channel_id=1, source_target_pairs={{0,16},{16,32},{32,48},{48,64},{64,80},{80,96},{96,112},{1,17},{17... | collective-permute-start | bytes 221192 | tf_op jit(solution)/shard_map/ppermute | solution.py:24
  68.3 6.6 %collective-permute-start.5 = (f32[1,24,6,128]{3,1,2,0:T(8,128)S(1)}, f32[1,24,6,128]{3,1,2,0:T(8,128)S(1)}, u32[]{:S(2)}, u32[]{:S(2)}) collective-permute-start(f32[1,24,6,128]{3,1,2,0:T(8,128)S(1)} %get-tuple-element.15), channel_id=1, source_target_pairs={{16,0},{32,16},{48,32},{64,48},{80,64},{96,80},{112,96},{17,1},{33... | collective-permute-start | bytes 221192 | tf_op jit(solution)/shard_map/ppermute | solution.py:26
  75.0 6.2 %collective-permute-start.6 = (f32[26,1,6,128]{3,1,2,0:T(1,128)S(1)}, f32[26,1,6,128]{3,1,2,0:T(1,128)S(1)}, u32[]{:S(2)}, u32[]{:S(2)}) collective-permute-start(f32[26,1,6,128]{3,1,2,0:T(1,128)S(1)} %get-tuple-element.10), channel_id=1, source_target_pairs={{0,1},{1,2},{2,3},{3,4},{4,5},{5,6},{6,7},{7,8},{8,9},{9,10},{10,1... | collective-permute-start | bytes 239624 | tf_op jit(solution)/shard_map/ppermute | solution.py:24
  78.6 5.7 %collective-permute-start.7 = (f32[26,1,6,128]{3,1,2,0:T(1,128)S(1)}, f32[26,1,6,128]{3,1,2,0:T(1,128)S(1)}, u32[]{:S(2)}, u32[]{:S(2)}) collective-permute-start(f32[26,1,6,128]{3,1,2,0:T(1,128)S(1)} %get-tuple-element.11), channel_id=1, source_target_pairs={{1,0},{2,1},{3,2},{4,3},{5,4},{6,5},{7,6},{8,7},{9,8},{10,9},{11,1... | collective-permute-start | bytes 239624 | tf_op jit(solution)/shard_map/ppermute | solution.py:26
  84.4 4.1 copy-start.8
Sparse Core Ops, SparseCore 0:
  94.7 152.5 all-reduce.1

commit v2 on v1

--- a/solution.py
+++ b/solution.py
@@ -5,46 +5,196 @@
 from jax.experimental.pallas import tpu as pltpu
 from jax.sharding import PartitionSpec as P
 
-STEPS = 2
 OB = 64
+MESH = pl.DeviceIdType.MESH
 ITERS = 5
 BOUND = 16.0
 F32 = jnp.float32
 BF16 = jnp.bfloat16
 
 
-def with_halo(cells, sides, width):
-    for axis, dim in sides:
-        count = lax.axis_size(axis)
-        ends = count - 1
-        head = lax.slice_in_dim(cells, 0, width, axis=dim)
-        tail = lax.slice_in_dim(cells, cells.shape[dim] - width, cells.shape[dim], axis=dim)
-        cells = jnp.concatenate(
-            [
-                lax.ppermute(tail, axis, [(i, (i + 1) % count) for i in range(ends)]),
-                cells,
-                lax.ppermute(head, axis, [((i + 1) % count, i) for i in range(ends)]),
-            ],
-            axis=dim,
+def forecast(x_ref, coef_ref, edge_ref, out_ref, mid_ref, cols_ref, rows_in, cols_in, send_sem, recv_sem):
+    strip, members = rows_in.shape[2:]
+    block_x, block_y = coef_ref.shape[:2]
+    levels = strip // block_y
+    gx, gy = lax.axis_index("gx"), lax.axis_index("gy")
+    nx, ny = lax.axis_size("gx"), lax.axis_size("gy")
+    west, east = (lax.rem(gx + nx - 1, nx), gy), (lax.rem(gx + 1, nx), gy)
+    south, north = (gx, lax.rem(gy + ny - 1, ny)), (gx, lax.rem(gy + 1, ny))
+    barrier = pltpu.get_barrier_semaphore()
+    for device in (west, east, south, north):
+        pl.semaphore_signal(barrier, inc=1, device_id=device, device_id_type=MESH)
+    from_west = jnp.where(gx > 0, 1.0, 0.0).astype(F32)
+    from_east = jnp.where(gx < nx - 1, 1.0, 0.0).astype(F32)
+    from_south = jnp.where(gy > 0, 1.0, 0.0).astype(F32)
+    from_north = jnp.where(gy < ny - 1, 1.0, 0.0).astype(F32)
+    count = block_x * levels
+
+    def pack(field, turn):
+        cols_ref[turn, 0] = field[pl.ds(0, count, stride=block_y), :]
+        cols_ref[turn, 1] = field[pl.ds(block_y - 1, count, stride=block_y), :]
+
+    def sends(field, turn):
+        last = (block_x - 1) * strip
+        plan = (
+            (field.at[pl.ds(last, strip)], rows_in.at[turn, 0], east),
+            (field.at[pl.ds(0, strip)], rows_in.at[turn, 1], west),
+            (cols_ref.at[turn, 1], cols_in.at[turn, 0], north),
+            (cols_ref.at[turn, 0], cols_in.at[turn, 1], south),
         )
-    return cells
-
-
-def propagate_prediction(bordered_grid, primary_cfl, secondary_cfl, spreading_rate):
-    centre = bordered_grid[1:-1, 1:-1]
-    west = bordered_grid[:-2, 1:-1]
-    east = bordered_grid[2:, 1:-1]
-    south = bordered_grid[1:-1, :-2]
-    north = bordered_grid[1:-1, 2:]
-    cxe = primary_cfl[..., None]
-    cye = secondary_cfl[..., None]
-    kde = spreading_rate[..., None]
-    tend = -(jnp.maximum(cxe, 0.0) * (centre - west) + jnp.minimum(cxe, 0.0) * (east - centre))
-    tend = tend - (
-        jnp.maximum(cye, 0.0) * (centre - south) + jnp.minimum(cye, 0.0) * (north - centre)
+        return [
+            pltpu.make_async_remote_copy(
+                src_ref=source,
+                dst_ref=target,
+                send_sem=send_sem.at[turn, i],
+                recv_sem=recv_sem.at[turn, i],
+                device_id=device,
+                device_id_type=MESH,
+            )
+            for i, (source, target, device) in enumerate(plan)
+        ]
+
+    def strip_of(field, i):
+        return [field[pl.ds(pl.multiple_of((i * levels + l) * block_y, block_y), block_y), :] for l in range(levels)]
+
+    def advance(i, centre, left, right, target):
+        coef = coef_ref[i]
+        for l in range(levels):
+            w = [jnp.broadcast_to(coef[:, k * levels + l : k * levels + l + 1], (block_y, members)) for k in range(5)]
+            c = centre[l]
+            new = w[0] * c + w[1] * left[l] + w[2] * right[l]
+            new = new + w[3] * pltpu.roll(c, 1, 0) + w[4] * pltpu.roll(c, block_y - 1, 0)
+            target[pl.ds(pl.multiple_of((i * levels + l) * block_y, block_y), block_y), :] = new
+
+    def turn_of(field, target, turn):
+        copies = sends(field, turn)
+        for copy in copies:
+            copy.start()
+
+        def inner(i, _):
+            advance(i, strip_of(field, i), strip_of(field, i - 1), strip_of(field, i + 1), target)
+            return 0
+
+        lax.fori_loop(1, block_x - 1, inner, 0)
+        copies[0].wait_recv()
+        left = [rows_in[turn, 0, pl.ds(l * block_y, block_y), :] * from_west for l in range(levels)]
+        advance(0, strip_of(field, 0), left, strip_of(field, 1), target)
+        copies[1].wait_recv()
+        right = [rows_in[turn, 1, pl.ds(l * block_y, block_y), :] * from_east for l in range(levels)]
+        last = block_x - 1
+        advance(last, strip_of(field, last), strip_of(field, last - 1), right, target)
+        edge = edge_ref[...]
+        for side, (at, here) in enumerate(((0, from_south), (block_y - 1, from_north))):
+            copies[2 + side].wait_recv()
+            rows = pl.ds(at, count, stride=block_y)
+            gain = jnp.broadcast_to(edge[:, side : side + 1] * here, (count, members))
+            target[rows, :] = target[rows, :] + gain * cols_in[turn, side]
+        return copies
+
+    pack(x_ref, 0)
+    pl.semaphore_wait(barrier, 4)
+    first = turn_of(x_ref, mid_ref, 0)
+    pack(mid_ref, 1)
+    second = turn_of(mid_ref, out_ref, 1)
+    for copy in first + second:
+        copy.wait_send()
+
+
+def collect(
+    order_ref, place_ref, scale_ref, fx_ref, fy_ref, ir_ref, shift_ref, field_ref, noise_ref,
+    y_ref, w_ref, rows_x, rows_y, rows_r, part_ref, half_ref, sum_ref, slots_ref, send_sem, recv_sem,
+):
+    count = part_ref.shape[0]
+    half = count // 2
+    gx, gy = lax.axis_index("gx"), lax.axis_index("gy")
+    nx, ny = lax.axis_size("gx"), lax.axis_size("gy") // 2
+    chips = nx * ny
+    piece = half // chips
+    core = lax.rem(gy, 2)
+    chip = gx * ny + gy // 2
+    partner = (gx, gy + 1 - 2 * core)
+
+    def device(t):
+        return (t // ny, lax.rem(t, ny) * 2 + core)
+
+    barrier = pltpu.get_barrier_semaphore()
+    pl.semaphore_signal(barrier, inc=1, device_id=partner, device_id_type=MESH)
+
+    def greet(k, _):
+        pl.semaphore_signal(barrier, inc=1, device_id=device(lax.rem(chip + k, chips)), device_id_type=MESH)
+        return 0
+
+    lax.fori_loop(1, chips, greet, 0)
+    wide = (1, part_ref.shape[1])
+
+    def pick(g, _):
+        for u in range(8):
+            k = g * 8 + u
+            o = order_ref[k]
+            part_ref[pl.ds(k, 1), :] = field_ref[pl.ds(place_ref[o], 1), :] * jnp.full(wide, scale_ref[o])
+        return 0
+
+    lax.fori_loop(0, count // 8, pick, 0)
+
+    def prepare(g, _):
+        for u in range(8):
+            k = g * 8 + u
+            o = order_ref[k]
+            at = pl.ds(k, 1)
+            w_ref[at, :] = noise_ref[pl.ds(o, 1), :] + jnp.full(wide, shift_ref[o])
+            rows_x[at, :] = jnp.full(wide, fx_ref[o])
+            rows_y[at, :] = jnp.full(wide, fy_ref[o])
+            rows_r[at, :] = jnp.full(wide, ir_ref[o])
+        return 0
+
+    groups = count // 8
+    pl.semaphore_wait(barrier, chips)
+    mine = pl.ds(pl.multiple_of(core * half, half), half)
+    other = pl.ds(pl.multiple_of((1 - core) * half, half), half)
+    swap = pltpu.make_async_remote_copy(
+        src_ref=part_ref.at[other], dst_ref=half_ref, send_sem=send_sem.at[0], recv_sem=recv_sem.at[0],
+        device_id=partner, device_id_type=MESH,
     )
-    tend = tend + kde * (east + west + north + south - 4.0 * centre)
-    return centre + tend
+    swap.start()
+    lax.fori_loop(0, groups // 8, prepare, 0)
+    swap.wait_recv()
+    sum_ref[...] = (part_ref[mine, :] + half_ref[...]).reshape(sum_ref.shape)
+
+    def scatter(k, _):
+        t = lax.rem(chip + k, chips)
+        pltpu.make_async_remote_copy(
+            src_ref=sum_ref.at[t], dst_ref=slots_ref.at[chip], send_sem=send_sem.at[1], recv_sem=recv_sem.at[1],
+            device_id=device(t), device_id_type=MESH,
+        ).start()
+        return 0
+
+    lax.fori_loop(1, chips, scatter, 0)
+    slots_ref[chip] = sum_ref[chip]
+    lax.fori_loop(groups // 8, groups // 2, prepare, 0)
+    some = slots_ref.at[pl.ds(0, chips - 1)]
+    pltpu.make_async_copy(some, some, recv_sem.at[1]).wait()
+    own = pl.ds(pl.multiple_of(core * half + chip * piece, piece), piece)
+    y_ref[own, :] = jnp.sum(slots_ref[...], axis=0)
+
+    def gather(k, _):
+        pltpu.make_async_remote_copy(
+            src_ref=y_ref.at[own], dst_ref=y_ref.at[own], send_sem=send_sem.at[2], recv_sem=recv_sem.at[2],
+            device_id=device(lax.rem(chip + k, chips)), device_id_type=MESH,
+        ).start()
+        return 0
+
+    lax.fori_loop(1, chips, gather, 0)
+    lax.fori_loop(groups // 2, groups, prepare, 0)
+    pltpu.make_async_copy(some, some, recv_sem.at[2]).wait()
+    share = pltpu.make_async_remote_copy(
+        src_ref=y_ref.at[mine], dst_ref=y_ref.at[mine], send_sem=send_sem.at[3], recv_sem=recv_sem.at[3],
+        device_id=partner, device_id_type=MESH,
+    )
+    share.start()
+    swap.wait_send()
+    pltpu.make_async_copy(some, some, send_sem.at[1]).wait()
+    pltpu.make_async_copy(some, some, send_sem.at[2]).wait()
+    share.wait()
 
 
 def split(x):
@@ -52,7 +202,7 @@
     return high, (x - high.astype(F32)).astype(BF16)
 
 
-def assimilate(fx_ref, fy_ref, ir_ref, rows_x, rows_y, y_in, w_ref, x_ref, out_ref, y_ref, t_ref, v_ref):
+def assimilate(rows_x, rows_y, rows_r, y_in, w_ref, x_ref, out_ref, y_ref, t_ref, v_ref):
     block_x, levels, block_y, members = x_ref.shape
     count = y_in.shape[0]
     batches = count // OB
@@ -129,9 +279,9 @@
             both = jnp.concatenate(split(g), axis=1)
             return jnp.dot(both, solved, preferred_element_type=F32)
 
-        px = fx_ref[pl.ds(b, 1), :]
-        py = fy_ref[pl.ds(b, 1), :]
-        ir = ir_ref[pl.ds(b, 1), :]
+        px = jnp.sum(rows_x[now, :] * eye, axis=0, keepdims=True)
+        py = jnp.sum(rows_y[now, :] * eye, axis=0, keepdims=True)
+        ir = jnp.sum(rows_r[now, :] * eye, axis=0, keepdims=True)
 
         def later(j, _):
             at = pl.ds(pl.multiple_of(j * OB, OB), OB)
@@ -176,54 +326,85 @@
     obs_noise,
 ):
     block_x, block_y, levels, members = ensemble.shape
-    current_vector = ensemble
-    for step in range(STEPS):
-        bordered_grid = with_halo(current_vector, (("gx", 0), ("gy", 1)), 1)
-        current_vector = propagate_prediction(
-            bordered_grid, cfl_ratio_primary_axis, cfl_ratio_secondary_axis, spreading_ratio
-        )
+    span_y = lax.axis_size("gy")
+    span = lax.axis_size("gx") * span_y
     row_index = lax.axis_index("gx")
     col_index = lax.axis_index("gy")
-    span_y = lax.axis_size("gy")
     myself = row_index * span_y + col_index
-    owner = obs_owner[batch_order]
-    local = obs_local[batch_order]
-    ix = local // (block_y * levels)
-    iy = local // levels % block_y
-    lev = local % levels
-    fx = (owner // span_y * block_x + ix - row_index * block_x).astype(F32)
-    fy = (owner % span_y * block_y + iy - col_index * block_y).astype(F32)
-    reach = obs_reach[batch_order].astype(F32)
-    count = local.shape[0]
-    batches = count // OB
-
-    def lanes(v):
-        v = v.reshape(batches, OB)
-        return jnp.concatenate([v, v], axis=1)
-
-    root = jnp.sqrt(obs_variance[batch_order])
-    inv = 1.0 / root
-    wanted = obs_noise[batch_order] + (obs_value[batch_order] * inv)[:, None]
-    state = jnp.transpose(current_vector, (0, 2, 1, 3))
-    flat = state.reshape(-1, members)
-    picked = jnp.take(flat, (ix * levels + lev) * block_y + iy, axis=0)
-    picked = picked * jnp.where(owner == myself, inv, 0.0)[:, None]
-    seen = lax.psum(picked, ("gx", "gy"))
-    args = (
-        lanes(fx),
-        lanes(fy),
-        lanes(1.0 / (reach * reach)),
-        jnp.broadcast_to(fx[:, None], (count, members)),
-        jnp.broadcast_to(fy[:, None], (count, members)),
-        seen,
-        wanted,
+    count = obs_local.shape[0]
+    size = block_x * levels * block_y
+    strip = levels * block_y
+    flat = jnp.transpose(ensemble, (0, 2, 1, 3)).reshape(size, members)
+    cx, cy, kd = cfl_ratio_primary_axis, cfl_ratio_secondary_axis, spreading_ratio
+    west = kd + jnp.maximum(cx, 0.0)
+    east = kd - jnp.minimum(cx, 0.0)
+    south = kd + jnp.maximum(cy, 0.0)
+    north = kd - jnp.minimum(cy, 0.0)
+    centre = 1.0 - (west + east + south + north)
+    spot = lax.broadcasted_iota(jnp.int32, cx.shape, 1)
+    inner_south = jnp.where(spot == 0, 0.0, south)
+    inner_north = jnp.where(spot == block_y - 1, 0.0, north)
+    coef = jnp.concatenate([centre, west, east, inner_south, inner_north], axis=2)
+    edge = jnp.stack([south[:, 0, :].reshape(-1), north[:, block_y - 1, :].reshape(-1)], axis=1)
+    vmem = pl.BlockSpec(memory_space=pltpu.VMEM)
+    smem = pl.BlockSpec(memory_space=pltpu.SMEM)
+    state = pl.pallas_call(
+        forecast,
+        out_shape=jax.ShapeDtypeStruct((size, members), F32),
+        in_specs=[vmem] * 3,
+        out_specs=vmem,
+        scratch_shapes=[
+            pltpu.VMEM((size, members), F32),
+            pltpu.VMEM((2, 2, block_x * levels, members), F32),
+            pltpu.VMEM((2, 2, strip, members), F32),
+            pltpu.VMEM((2, 2, block_x * levels, members), F32),
+            pltpu.SemaphoreType.DMA((2, 4)),
+            pltpu.SemaphoreType.DMA((2, 4)),
+        ],
+        compiler_params=pltpu.CompilerParams(collective_id=0, has_side_effects=True),
+        name="forecast",
+    )(flat, coef, edge)
+    ix = obs_local // (block_y * levels)
+    iy = obs_local // levels % block_y
+    lev = obs_local % levels
+    fx = (obs_owner // span_y * block_x + ix - row_index * block_x).astype(F32)
+    fy = (obs_owner % span_y * block_y + iy - col_index * block_y).astype(F32)
+    reach = obs_reach.astype(F32)
+    inv = lax.rsqrt(obs_variance)
+    pieces = span // 2
+    table = jax.ShapeDtypeStruct((count, members), F32)
+    seen, wanted, rows_x, rows_y, rows_r = pl.pallas_call(
+        collect,
+        out_shape=[table] * 5,
+        in_specs=[smem] * 7 + [vmem] * 2,
+        out_specs=[vmem] * 5,
+        scratch_shapes=[
+            pltpu.VMEM((count, members), F32),
+            pltpu.VMEM((count // 2, members), F32),
+            pltpu.VMEM((pieces, count // span, members), F32),
+            pltpu.VMEM((pieces, count // span, members), F32),
+            pltpu.SemaphoreType.DMA((4,)),
+            pltpu.SemaphoreType.DMA((4,)),
+        ],
+        compiler_params=pltpu.CompilerParams(collective_id=1, has_side_effects=True),
+        name="collect",
+    )(
+        batch_order,
+        (ix * levels + lev) * block_y + iy,
+        jnp.where(obs_owner == myself, inv, 0.0),
+        fx,
+        fy,
+        1.0 / (reach * reach),
+        obs_value * inv,
         state,
+        obs_noise,
     )
+    args = (rows_x, rows_y, rows_r, seen, wanted, state.reshape(block_x, levels, block_y, members))
     out = pl.pallas_call(
         assimilate,
-        out_shape=jax.ShapeDtypeStruct(state.shape, F32),
-        in_specs=[pl.BlockSpec(memory_space=pltpu.VMEM)] * len(args),
-        out_specs=pl.BlockSpec(memory_space=pltpu.VMEM),
+        out_shape=jax.ShapeDtypeStruct((block_x, levels, block_y, members), F32),
+        in_specs=[vmem] * len(args),
+        out_specs=vmem,
         scratch_shapes=[
             pltpu.VMEM((count, members), F32),
             pltpu.VMEM((OB, 2 * OB), F32),

time: 451 us -> 252 us (0.56)
  waiting for transfers between devices: 159 us -> 0 us
  Pallas kernels: 194 us -> 243 us
  local copies, waits for them, and re-layouts: 34.8 us -> 5.38 us
  starting transfers between devices: 25.3 us -> 0 us
  other arithmetic: 23.3 us -> 2.89 us
  between operations: 13.8 us -> 0.05 us
    psum x1 -> x0, waiting for transfers between devices: 148 us -> none  [per_device(): seen = lax.psum(picked, ('gx', 'gy'))]
    pallas_call x1 -> x3, Pallas kernels: 194 us -> 243 us  [the longest x1 194 us: per_device(): pl.pallas_call(assimilate, out_shape=jax.ShapeDtypeStruct((block_x, level...]
    gather x8 -> x0, local copies, waits for them, and re-layouts: 29.8 us -> none  [the longest x2 7.33 us: per_device(): wanted = obs_noise[batch_order] + (obs_value[batch_order] * inv)[:, None]]
    ppermute x8 -> x0, starting transfers between devices: 25.3 us -> none  [the longest x4 18.9 us: with_halo(): lax.ppermute(tail, axis, [(i, (i + 1) % count) for i in range(ends)])]
    add x3 -> x0, other arithmetic: 11.7 us -> none  [the longest x2 10.7 us: propagate_prediction(): return centre + tend]
    ppermute x8 -> x0, waiting for transfers between devices: 11.3 us -> none  [the longest x4 11.3 us: with_halo(): lax.ppermute(head, axis, [((i + 1) % count, i) for i in range(ends)])]
    transpose x1 -> x0, other arithmetic: 5.09 us -> none  [per_device(): state = jnp.transpose(current_vector, (0, 2, 1, 3))]
  transfers between devices with their start and end apart: 9 -> 0, of which waited for: 4 -> 0; matrix products, arithmetic and copies ran while one was open for 8% -> 0% of each run, Pallas kernels for 0% -> 0%
where the time goes in v2:
time: 252 us; the launch traced here: 251 us
  Pallas kernels  243 us (96%)
  local copies, waits for them, and re-layouts  5.38 us (2%)
  other arithmetic  2.89 us (1%)
    pallas_call x1, Pallas kernels, per_device(): pl.pallas_call(assimilate, out_shape=jax.ShapeDtypeStruct((block_x, level...  194 us
    pallas_call x1, Pallas kernels, per_device(): pl.pallas_call(collect, out_shape=[table] * 5, in_specs=[smem] * 7 + [vme...  28.3 us
    pallas_call x1, Pallas kernels, per_device(): pl.pallas_call(forecast, out_shape=jax.ShapeDtypeStruct((size, members),...  20.8 us

profile of v2, /device:TPU:1, one launch (start us, length us, event | category | flops | bytes accessed | tf_op | source)
XLA Modules:
  0.0 251.2 jit_solution(12392334193175181332)
XLA Ops:
  0.0 1.3 fusion.11
  1.3 1.3 rsqrt_multiply_fusion
  2.7 1.1 copy.40
  3.8 1.1 copy.39
  4.9 1.1 copy.43
  6.0 0.1 broadcast_select_fusion.1
  6.1 0.1 slice_reduce_fusion
  6.2 0.1 add_subtract_fusion
  6.3 1.1 concatenate.3.coef_ref
  7.3 0.1 stack_reshape_squeeze.7
  7.4 0.1 stack_reshape_squeeze.6
  7.6 0.7 copy.48.edge_ref
  8.3 20.8 %forecast.1.field_ref = f32[3456,128]{1,0:T(8,128)} custom-call(f32[3456,128]{1,0:T(8,128)} %bitcast.6, f32[24,24,30]{2,1,0:T(8,128)} %concatenate.3.coef_ref, f32[144,2]{1,0:T(8,128)} %copy.48.edge_ref), custom_call_target="tpu_custom_call" | custom-call | tf_op jit(solution)/shard_map/forecast/pallas_call | solution.py:351
  29.1 28.3 %collect.1 = (f32[1024,128]{1,0:T(8,128)}, f32[1024,128]{1,0:T(8,128)}, f32[1024,128]{1,0:T(8,128)}, f32[1024,128]{1,0:T(8,128)}, f32[1024,128]{1,0:T(8,128)}) custom-call(s32[1024]{0:T(1024)} %order_ref.1, s32[1024]{0:T(1024)} %get-tuple-element.28.place_ref, f32[1024]{0:T(1024)} %get-tuple-element.27.scale_ref, f32[1024]{0:T(1024)} %get-tuple-element.25.fx_ref, ...), custom_call_target="tpu_custom_call" | custom-call | tf_op jit(solution)/shard_map/collect/pallas_call | solution.py:376
  57.4 193.8 %assimilate.1 = f32[24,6,24,128]{3,2,1,0:T(8,128)} custom-call(f32[1024,128]{1,0:T(8,128)} %get-tuple-element.10.rows_x, f32[1024,128]{1,0:T(8,128)} %get-tuple-element.11.rows_y, f32[1024,128]{1,0:T(8,128)} %get-tuple-element.12.rows_r, f32[1024,128]{1,0:T(8,128)} %get-tuple-element.13.y_in, f32[1024,128]{1,0:T(8,128)} %get-tuple-element.14.w_ref, ...), custom_call_target="tpu_custom_call" | custom-call | tf_op jit(solution)/shard_map/assimilate/pallas_call | solution.py:403
  (3 shorter events, 0.0 us)

commit v3 on v2

--- a/solution.py
+++ b/solution.py
@@ -1,3 +1,5 @@
+import functools
+
 import jax
 import jax.numpy as jnp
 from jax import lax
@@ -6,9 +8,10 @@
 from jax.sharding import PartitionSpec as P
 
 OB = 64
+QUICK = 6.5
+WIDE = 63.0
+LONG = 6
 MESH = pl.DeviceIdType.MESH
-ITERS = 5
-BOUND = 16.0
 F32 = jnp.float32
 BF16 = jnp.bfloat16
 
@@ -202,114 +205,212 @@
     return high, (x - high.astype(F32)).astype(BF16)
 
 
-def assimilate(rows_x, rows_y, rows_r, y_in, w_ref, x_ref, out_ref, y_ref, t_ref, v_ref):
+def wide(x):
+    return jnp.concatenate(split(x), axis=1)
+
+
+def project(side, x):
+    pair = lax.dot_general(wide(x), side, (((1,), (1,)), ((), ())), preferred_element_type=F32)
+    half = pair.shape[1] // 2
+    return pair[:, :half] + pair[:, half:]
+
+
+def spread(solved, g):
+    return jnp.dot(wide(g), solved, preferred_element_type=F32)
+
+
+def stack_solved(v, scale):
+    high, low = split(v * scale)
+    return jnp.concatenate([high, low, high, low], axis=0)
+
+
+def sharpen(r, v, t, eye, last):
+    t = 2.0 * t * t - 1.0
+    back = 1.0 / t
+    gain = 1.0 + back
+    rh, rl = split(r)
+    vh, vl = split(v)
+    left = jnp.concatenate([rh, rl], axis=1)
+    head = jnp.concatenate([rh, vh], axis=1)
+    tail = jnp.concatenate([rl, vl], axis=1)
+    right = jnp.concatenate([head, tail, head, tail], axis=0)
+    prod = jnp.dot(left, right, preferred_element_type=F32)
+    v = gain * (v + prod[:, 2 * OB :])
+    r = None if last else gain * prod[:, : 2 * OB] - back * eye
+    return r, v, t
+
+
+def begin(p, rhs, norm, eye):
+    c = 1.0 + jnp.maximum(norm, 0.0625)
+    top = c + 1.0
+    alpha = 2.0 / top
+    return ((c - 1.0) / top) * eye - alpha * p, alpha * rhs, top / (c - 1.0)
+
+
+def assimilate(
+    rows_x, rows_y, rows_r, y_in, w_ref, x_ref, out_ref, y_ref, t_ref, v_ref, cur_ref, side_ref, solved_ref, lanes_ref
+):
     block_x, levels, block_y, members = x_ref.shape
     count = y_in.shape[0]
     batches = count // OB
+    scale = 1.0 / (members - 1.0)
     y_ref[...] = y_in[...]
     out_ref[...] = x_ref[...]
+    cur_ref[...] = y_in[pl.ds(0, OB), :]
+    side_ref[...] = jnp.zeros_like(side_ref)
+    solved_ref[...] = jnp.zeros_like(solved_ref)
+    lanes_ref[...] = jnp.zeros_like(lanes_ref)
     lane = lax.broadcasted_iota(jnp.int32, (OB, 2 * OB), 1)
     row = lax.broadcasted_iota(jnp.int32, (OB, 2 * OB), 0)
     eye = jnp.where((lane == row) | (lane == row + OB), 1.0, 0.0).astype(F32)
     ys = lax.broadcasted_iota(jnp.int32, (block_y, 1), 0).astype(F32)
 
-    def step(b, _):
+    def rho_rows(at, px, py, ir):
+        dx = rows_x[at, :] - px
+        dy = rows_y[at, :] - py
+        near = jnp.maximum(1.0 - (dx * dx + dy * dy) * ir, 0.0)
+        return near * near
+
+    def cells(n, side, solved, px, dy2, ir):
+        rhos = []
+        for u in range(6):
+            dx = jnp.float32(1.0) * (n * 6 + u) - px
+            near = jnp.maximum((1.0 - dx * dx * ir) - dy2, 0.0)
+            rhos.append((near * near)[None, None])
+        rho = jnp.concatenate(rhos, axis=0)
+        at = pl.ds(n * 6, 6)
+        old = out_ref[at].reshape(6 * levels * block_y, members)
+        g = project(side, old).reshape(6, levels, block_y, members) * rho
+        new = old + spread(solved, g.reshape(6 * levels * block_y, members))
+        out_ref[at] = new.reshape(6, levels, block_y, members)
+
+    def previous():
+        px, py, ir = lanes_ref[pl.ds(0, 1), :], lanes_ref[pl.ds(1, 1), :], lanes_ref[pl.ds(2, 1), :]
+        dy = ys - py
+        return side_ref[...], solved_ref[...], px, py, dy * dy * ir, ir
+
+    def step(first, b, _):
         now = pl.ds(pl.multiple_of(b * OB, OB), OB)
-        hx = y_ref[now, :]
+        after = pl.ds(pl.multiple_of(jnp.minimum(b + 1, batches - 1) * OB, OB), OB)
+        side0, solved0, px0, py0, dy20, ir0 = previous()
+
+        def later(start, size):
+            at = pl.ds(start, size)
+            old = y_ref[at, :]
+            y_ref[at, :] = old + spread(solved0, project(side0, old) * rho_rows(at, px0, py0, ir0))
+
+        pieces = []
+        for start in range((first + 1) * OB, count, 384):
+            pieces.append(functools.partial(later, start, min(384, count - start)))
+        ahead_of = len(pieces)
+        for n in range(block_x // 6):
+            pieces.append(functools.partial(cells, n, side0, solved0, px0, dy20, ir0))
+        plan = list([0.15, 0.3, 0.45, 0.6, 0.75, 0.9, 1])
+        total = len(pieces)
+        done = [0]
+
+        def fill():
+            share = plan.pop(0)
+            upto = total if not plan else min(total, round(share * total))
+            while done[0] < upto:
+                pieces[done[0]]()
+                done[0] += 1
+
+        hx = cur_ref[...]
         centred = hx - jnp.mean(hx, axis=1, keepdims=True)
         high, low = split(centred)
         high2 = jnp.concatenate([high, high], axis=1)
         low2 = jnp.concatenate([low, low], axis=1)
         side = jnp.concatenate([high2, low2, low2, high2], axis=0)
-
-        def project(x):
-            both = jnp.concatenate(split(x), axis=1)
-            pair = lax.dot_general(both, side, (((1,), (1,)), ((), ())), preferred_element_type=F32)
-            return pair[:, : 2 * OB] + pair[:, 2 * OB :]
-
-        p = project(centred) * (1.0 / (members - 1.0))
+        fill()
+        p = project(side, centred) * scale
+        fill()
         norm = jnp.max(jnp.sum(jnp.abs(p), axis=0, keepdims=True), axis=1, keepdims=True)
-        c = 1.0 + jnp.maximum(norm, 0.0625)
-        top = c + 1.0
-        t = top / (c - 1.0)
-        alpha = 2.0 / top
-        r = ((c - 1.0) / top) * eye - alpha * p
         rhs = w_ref[now, :] - hx
-        v = alpha * rhs
-        for i in range(ITERS):
-            t = 2.0 * t * t - 1.0
-            back = 1.0 / t
-            gain = 1.0 + back
-            rh, rl = split(r)
-            vh, vl = split(v)
-            left = jnp.concatenate([rh, rl], axis=1)
-            head = jnp.concatenate([rh, vh], axis=1)
-            tail = jnp.concatenate([rl, vl], axis=1)
-            right = jnp.concatenate([head, tail, head, tail], axis=0)
-            prod = jnp.dot(left, right, preferred_element_type=F32)
-            v = gain * (v + prod[:, 2 * OB :])
-            if i + 1 < ITERS:
-                r = gain * prod[:, : 2 * OB] - back * eye
-        v_ref[...] = v
-
-        @pl.when(jnp.max(norm) > BOUND)
+        r, v, t = begin(p, rhs, norm, eye)
+        for i in range(4):
+            r, v, t = sharpen(r, v, t, eye, i + 1 == 4)
+            fill()
+            if i == 4 - 2:
+                while done[0] < ahead_of:
+                    pieces[done[0]]()
+                    done[0] += 1
+                ahead = y_ref[after, :]
+                px = jnp.sum(rows_x[now, :] * eye, axis=0, keepdims=True)
+                py = jnp.sum(rows_y[now, :] * eye, axis=0, keepdims=True)
+                ir = jnp.sum(rows_r[now, :] * eye, axis=0, keepdims=True)
+                g = project(side, ahead) * rho_rows(after, px, py, ir)
+        new_solved = stack_solved(v, scale)
+        fresh = ahead + spread(new_solved, g)
+        fill()
+        side_ref[...] = side
+        solved_ref[...] = new_solved
+        lanes_ref[pl.ds(0, 1), :] = px
+        lanes_ref[pl.ds(1, 1), :] = py
+        lanes_ref[pl.ds(2, 1), :] = ir
+        cur_ref[...] = fresh
+
+        @pl.when(jnp.max(norm) > QUICK)
         def _():
             t_ref[...] = p + eye
             v_ref[...] = rhs
 
-            def pivot(k, _):
-                at = lane[:1, :] == k
-                trow = t_ref[pl.ds(k, 1), :]
-                scale = 1.0 / jnp.sum(jnp.where(at, trow, 0.0), axis=1, keepdims=True)
-                trow = trow * scale
-                vrow = v_ref[pl.ds(k, 1), :] * scale
-                mat = t_ref[...]
-                col = jnp.sum(jnp.where(lane == k, mat, 0.0), axis=1, keepdims=True)
-                mine = row == k
-                t_ref[...] = jnp.where(mine, trow, mat - col * trow)
-                v_ref[...] = jnp.where(mine, vrow, v_ref[...] - col * vrow)
-                return 0
-
-            lax.fori_loop(0, OB, pivot, 0)
-
-        zh, zl = split(v_ref[...] * (1.0 / (members - 1.0)))
-        solved = jnp.concatenate([zh, zl, zh, zl], axis=0)
-
-        def spread(g):
-            both = jnp.concatenate(split(g), axis=1)
-            return jnp.dot(both, solved, preferred_element_type=F32)
-
-        px = jnp.sum(rows_x[now, :] * eye, axis=0, keepdims=True)
-        py = jnp.sum(rows_y[now, :] * eye, axis=0, keepdims=True)
-        ir = jnp.sum(rows_r[now, :] * eye, axis=0, keepdims=True)
-
-        def later(j, _):
-            at = pl.ds(pl.multiple_of(j * OB, OB), OB)
-            old = y_ref[at, :]
-            dx = rows_x[at, :] - px
-            dy = rows_y[at, :] - py
-            near = jnp.maximum(1.0 - (dx * dx + dy * dy) * ir, 0.0)
-            y_ref[at, :] = old + spread(project(old) * (near * near))
-            return 0
-
-        lax.fori_loop(b + 1, batches, later, 0)
-        dy = ys - py
-        dy2 = dy * dy * ir
-
-        def cells(i, _):
-            dx = i.astype(F32) - px
-            near = jnp.maximum((1.0 - dx * dx * ir) - dy2, 0.0)
-            rho = near * near
-            old = out_ref[i].reshape(levels * block_y, members)
-            g = project(old).reshape(levels, block_y, members) * rho[None]
-            new = old + spread(g.reshape(levels * block_y, members))
-            out_ref[i] = new.reshape(levels, block_y, members)
-            return 0
-
-        lax.fori_loop(0, block_x, cells, 0)
-        return 0
-
-    lax.fori_loop(0, batches, step, 0)
+            @pl.when(jnp.max(norm) <= WIDE)
+            def _():
+                r, v, t = begin(p, rhs, norm, eye)
+                for i in range(LONG):
+                    r, v, t = sharpen(r, v, t, eye, i + 1 == LONG)
+                v_ref[...] = v
+
+            @pl.when(jnp.max(norm) > WIDE)
+            def _():
+                lax.fori_loop(0, OB, pivot, 0)
+
+            exact = stack_solved(v_ref[...], scale)
+            solved_ref[...] = exact
+            cur_ref[...] = ahead + spread(exact, g)
+
+        return 0
+
+    def pivot(k, _):
+        trow = t_ref[pl.ds(k, 1), :]
+        here = lane[:1, :] == k
+        inverse = 1.0 / jnp.sum(jnp.where(here, trow, 0.0), axis=1, keepdims=True)
+        trow = trow * inverse
+        vrow = v_ref[pl.ds(k, 1), :] * inverse
+        mat = t_ref[...]
+        col = jnp.sum(jnp.where(lane == k, mat, 0.0), axis=1, keepdims=True)
+        mine = row == k
+        t_ref[...] = jnp.where(mine, trow, mat - col * trow)
+        v_ref[...] = jnp.where(mine, vrow, v_ref[...] - col * vrow)
+        return 0
+
+    for first in range(0, batches, 4):
+        lax.fori_loop(first, min(first + 4, batches), functools.partial(step, first), 0)
+    side, solved, px, _, dy2, ir = previous()
+    for n in range(block_x // 6):
+        cells(n, side, solved, px, dy2, ir)
+
+
+def run_assimilate(*args):
+    vmem = pl.BlockSpec(memory_space=pltpu.VMEM)
+    count, members = args[0].shape
+    return pl.pallas_call(
+        assimilate,
+        out_shape=jax.ShapeDtypeStruct(args[-1].shape, F32),
+        in_specs=[vmem] * len(args),
+        out_specs=vmem,
+        scratch_shapes=[
+            pltpu.VMEM((count, members), F32),
+            pltpu.VMEM((OB, 2 * OB), F32),
+            pltpu.VMEM((OB, members), F32),
+            pltpu.VMEM((OB, members), F32),
+            pltpu.VMEM((4 * OB, 2 * members), BF16),
+            pltpu.VMEM((4 * OB, members), BF16),
+            pltpu.VMEM((8, members), F32),
+        ],
+        name="assimilate",
+    )(*args)
 
 
 def per_device(
@@ -399,19 +500,9 @@
         state,
         obs_noise,
     )
-    args = (rows_x, rows_y, rows_r, seen, wanted, state.reshape(block_x, levels, block_y, members))
-    out = pl.pallas_call(
-        assimilate,
-        out_shape=jax.ShapeDtypeStruct((block_x, levels, block_y, members), F32),
-        in_specs=[vmem] * len(args),
-        out_specs=vmem,
-        scratch_shapes=[
-            pltpu.VMEM((count, members), F32),
-            pltpu.VMEM((OB, 2 * OB), F32),
-            pltpu.VMEM((OB, members), F32),
-        ],
-        name="assimilate",
-    )(*args)
+    out = run_assimilate(
+        rows_x, rows_y, rows_r, seen, wanted, state.reshape(block_x, levels, block_y, members)
+    )
     return jnp.transpose(out, (0, 2, 1, 3))
 
 

time: 252 us -> 95.4 us (0.38)
  Pallas kernels: 243 us -> 86.2 us
    pallas_call x1, Pallas kernels: 194 us -> 37.1 us  [run_assimilate(): pl.pallas_call(assimilate, out_shape=jax.ShapeDtypeStruct(args[-1].shape,...]
where the time goes in v3:
time: 95.4 us; the launch traced here: 94.5 us
  Pallas kernels  86.2 us (90%)
  local copies, waits for them, and re-layouts  5.38 us (6%)
  other arithmetic  2.89 us (3%)
    pallas_call x1, Pallas kernels, run_assimilate(): pl.pallas_call(assimilate, out_shape=jax.ShapeDtypeStruct(args[-1].shape,...  37.1 us
    pallas_call x1, Pallas kernels, per_device(): pl.pallas_call(collect, out_shape=[table] * 5, in_specs=[smem] * 7 + [vme...  28.3 us
    pallas_call x1, Pallas kernels, per_device(): pl.pallas_call(forecast, out_shape=jax.ShapeDtypeStruct((size, members),...  20.8 us
    unnamed x3, local copies, waits for them, and re-layouts  3.29 us

profile of v3, /device:TPU:1, one launch (start us, length us, event | category | flops | bytes accessed | tf_op | source)
XLA Modules:
  0.0 94.5 jit_solution(6259001092836846649)
XLA Ops:
  0.0 1.3 %fusion.11 = (f32[1024]{0:T(1024)}, f32[1024]{0:T(1024)}, s32[1024]{0:T(1024)}) fusion(s32[1024]{0:T(1024)} %param.15, s32[]{:T(128)S(6)} %mul.37, s32[1024]{0:T(1024)} %param.16, s32[]{:T(128)S(6)} %mul.35), kind=kLoop, calls=%fused_computation.29 | loop fusion | flops 56320 | bytes 20488 | tf_op jit(solution)/shard_map/convert_element_type | solution.py:472
  1.3 1.3 %rsqrt_multiply_fusion = (f32[1024]{0:T(1024)}, f32[1024]{0:T(1024)}, f32[1024]{0:T(1024)}) fusion(f32[1024]{0:T(1024)} %param.19, f32[1024]{0:T(1024)} %param.20, s32[1024]{0:T(1024)} %param.15, s32[]{:T(128)S(6)} %add.51, s32[1024]{0:T(1024)} %param.18), kind=kLoop, calls=%fused_computation.37 | loop fusion | flops 6144 | bytes 28676 | tf_op jit(solution)/shard_map/mul | solution.py:499
  2.7 1.1 %copy.40 = f32[24,24,6]{2,1,0:T(8,128)S(1)} copy(f32[24,24,6]{1,0,2:T(8,128)} %param.14) | data formatting | bytes 27648 | tf_op args[3]
  3.8 1.1 %copy.39 = f32[24,24,6]{2,1,0:T(8,128)S(1)} copy(f32[24,24,6]{1,0,2:T(8,128)} %param.12) | data formatting | bytes 27648 | tf_op args[1]
  4.9 1.1 %copy.43 = f32[24,24,6]{2,1,0:T(8,128)S(1)} copy(f32[24,24,6]{1,0,2:T(8,128)} %param.13) | data formatting | bytes 27648 | tf_op args[2]
  6.0 0.1 broadcast_select_fusion.1
  6.1 0.1 slice_reduce_fusion
  6.2 0.1 add_subtract_fusion
  6.3 1.1 %concatenate.3.coef_ref = f32[24,24,30]{2,1,0:T(8,128)} concatenate(f32[24,24,6]{2,1,0:T(8,128)S(1)} %get-tuple-element.19, f32[24,24,6]{2,1,0:T(8,128)S(1)} %get-tuple-element.21, f32[24,24,6]{2,1,0:T(8,128)S(1)} %get-tuple-element.20, f32[24,24,6]{2,1,0:T(8,128)S(1)} %get-tuple-element.17, f32[24,24,6]{2,1,0:T(8,128)S(1)} %get-tuple-element.22), dimensions={2} | concatenate | bytes 138240 | tf_op jit(solution)/shard_map/concatenate | solution.py:448
  7.3 0.1 stack_reshape_squeeze.7
  7.4 0.1 stack_reshape_squeeze.6
  7.6 0.7 copy.48.edge_ref
  8.3 20.8 %forecast.1.field_ref = f32[3456,128]{1,0:T(8,128)} custom-call(f32[3456,128]{1,0:T(8,128)} %bitcast.6, f32[24,24,30]{2,1,0:T(8,128)} %concatenate.3.coef_ref, f32[144,2]{1,0:T(8,128)} %copy.48.edge_ref), custom_call_target="tpu_custom_call" | custom-call | tf_op jit(solution)/shard_map/forecast/pallas_call | solution.py:452
  29.1 28.3 %collect.1 = (f32[1024,128]{1,0:T(8,128)}, f32[1024,128]{1,0:T(8,128)}, f32[1024,128]{1,0:T(8,128)}, f32[1024,128]{1,0:T(8,128)}, f32[1024,128]{1,0:T(8,128)}) custom-call(s32[1024]{0:T(1024)} %order_ref.1, s32[1024]{0:T(1024)} %get-tuple-element.28.place_ref, f32[1024]{0:T(1024)} %get-tuple-element.27.scale_ref, f32[1024]{0:T(1024)} %get-tuple-element.25.fx_ref, ...), custom_call_target="tpu_custom_call" | custom-call | tf_op jit(solution)/shard_map/collect/pallas_call | solution.py:477
  57.4 37.1 %assimilate.1 = f32[24,6,24,128]{3,2,1,0:T(8,128)} custom-call(f32[1024,128]{1,0:T(8,128)} %get-tuple-element.10.rows_x, f32[1024,128]{1,0:T(8,128)} %get-tuple-element.11.rows_y, f32[1024,128]{1,0:T(8,128)} %get-tuple-element.12.rows_r, f32[1024,128]{1,0:T(8,128)} %get-tuple-element.13.y_in, f32[1024,128]{1,0:T(8,128)} %get-tuple-element.14.w_ref, ...), custom_call_target="tpu_custom_call" | custom-call | tf_op jit(solution)/shard_map/assimilate/pallas_call | solution.py:398
  (3 shorter events, 0.0 us)
